TPU v7x, 32 devices: a whole 2x2x4 slice. The times are simulated.
32 devices in a mesh: groups: 2 (over x), dp: 4 (over y, core), region: 4 (over z).
Axes of the slice: x: 2, y: 2, z: 4, core: 2. Of those that a mesh axis runs over, the one named last changes fastest.
Arguments:
- features: bfloat16 [8, 16384, 256], P(('groups', 'dp'), 'region'), parts along dimension 0, may hold values from -6 to 6
- adjacency: bfloat16 [8, 384, 128, 128], P(('groups', 'dp'), 'region'), parts along dimension 0, may hold values from -0.3125 to 0.3125
- src_tiles: int32 [8, 384], P(('groups', 'dp'), 'region'), parts along dimension 0, may hold values from 0 to 39, as said below
- dst_tiles: int32 [8, 384], P(('groups', 'dp'), 'region'), parts along dimension 0, may hold values from 0 to 31
- counts: int32 [8, 4], P(('groups', 'dp'), 'region'), parts along dimension 0, may hold values from 1 to 96, as said below
- send_low: int32 [8, 16], P(('groups', 'dp'), 'region'), parts along dimension 0, may hold values from 0 to 31, as said below
- send_high: int32 [8, 16], P(('groups', 'dp'), 'region'), parts along dimension 0, may hold values from 0 to 31, as said below
- w_message: bfloat16 [256, 256], replicated, may hold values from -0.375 to 0.375
- w_update: bfloat16 [256, 256], replicated, may hold values from -0.375 to 0.375
- grad_out: bfloat16 [8, 16384, 256], P(('groups', 'dp'), 'region'), parts along dimension 0, may hold values from -6 to 6
Outputs:
- output: bfloat16 [8, 16384, 256], P(('groups', 'dp'), 'region'), parts along dimension 0
- grad_features: bfloat16 [8, 16384, 256], P(('groups', 'dp'), 'region'), parts along dimension 0
- grad_message: float32 [512, 256], P('groups'), parts along dimension 0
- grad_update: float32 [512, 256], P('groups'), parts along dimension 0
There are 2 independent parts, one for each index of `groups`. A program takes and returns all parts, laid end to end along the dimension named above; an argument that names none is the same for every part. Nothing has to cross between parts.
Inputs may be any that keep to these rules, and one draw needn't show every extreme that they name: `src_tiles`: index into a region's extended list of 40 tiles. `counts`: in each event one region has all 96 slots live. `send_low`: the 4 entries of one region are distinct. `send_high`: the 4 entries of one region are distinct.
All inputs are finite; a program needn't handle non-finite values.
Results may differ from a plain program's by a relative error of at most 0.007.
Values may be sent and summed in bfloat16 or wider, within the bound.
A program may use at most 128 MiB of HBM per device.

v0:
```python
import math
import jax
import jax.numpy as jnp
from jax import lax
from jax.sharding import PartitionSpec as P


def with_halo(cells, sides, width):
    for axis, dim in sides:
        count = lax.axis_size(axis)
        head = lax.slice_in_dim(cells, 0, width, axis=dim)
        tail = lax.slice_in_dim(cells, cells.shape[dim] - width, cells.shape[dim], axis=dim)
        cells = jnp.concatenate(
            [
                lax.ppermute(tail, axis, [(i, (i + 1) % count) for i in range(count)]),
                cells,
                lax.ppermute(head, axis, [((i + 1) % count, i) for i in range(count)]),
            ],
            axis=dim,
        )
    return cells


def body(
    features,
    adjacency,
    src_tiles,
    dst_tiles,
    counts,
    send_low,
    send_high,
    w_message,
    w_update,
    grad_out,
):
    tile = adjacency.shape[-1]
    slots = adjacency.shape[1]
    width = features.shape[-1]
    x_rows = features[0]
    ntile = x_rows.shape[0] // tile
    bound = send_low.shape[1]
    lows = send_low[0]
    highs = send_high[0]
    message = jnp.dot(x_rows, w_message, preferred_element_type=jnp.float32).astype(jnp.bfloat16)
    msg_tiles = message.reshape(ntile, tile, width)
    rims = jnp.concatenate([msg_tiles[lows], msg_tiles[highs]], axis=0)
    padded = with_halo(rims, (("region", 0),), bound)
    halo_tiles = jnp.concatenate([padded[:bound], padded[-bound:]], axis=0)
    extended = jnp.concatenate([msg_tiles, halo_tiles], axis=0)
    live = (jnp.arange(slots) < counts[0, 0]).astype(jnp.float32)
    src = src_tiles[0]
    dst = dst_tiles[0]
    adj = adjacency[0]
    gathered = extended[src]
    contrib = jnp.einsum("kij,kjd->kid", adj, gathered, preferred_element_type=jnp.float32)
    aggregate = (
        jnp.zeros((ntile, tile, width), jnp.float32).at[dst].add(contrib * live[:, None, None])
    )
    aggregate = aggregate.astype(jnp.bfloat16).reshape(-1, width)
    update = jnp.dot(aggregate, w_update, preferred_element_type=jnp.float32)
    sig = jax.nn.sigmoid(update)
    output = (x_rows.astype(jnp.float32) + update * sig).astype(jnp.bfloat16)
    g_rows = grad_out[0]
    grad_in = (g_rows.astype(jnp.float32) * sig * (1.0 + update * (1.0 - sig))).astype(jnp.bfloat16)
    part_update = lax.dot_general(
        aggregate, grad_in, (((0,), (0,)), ((), ())), preferred_element_type=jnp.float32
    )
    grad_agg = lax.dot_general(
        grad_in, w_update, (((1,), (1,)), ((), ())), preferred_element_type=jnp.float32
    )
    grad_agg = grad_agg.astype(jnp.bfloat16).reshape(ntile, tile, width)
    picked = grad_agg[dst]
    back = jnp.einsum("kij,kid->kjd", adj, picked, preferred_element_type=jnp.float32)
    grad_ext = (
        jnp.zeros((ntile + 2 * bound, tile, width), jnp.float32)
        .at[src]
        .add(back * live[:, None, None])
    )
    rims_back = grad_ext[ntile:]
    padded_back = with_halo(rims_back, (("region", 0),), bound)
    from_lower = padded_back[:bound]
    from_upper = padded_back[-bound:]
    grad_msg = grad_ext[:ntile]
    grad_msg = grad_msg.at[lows].add(from_lower)
    grad_msg = grad_msg.at[highs].add(from_upper)
    grad_msg = grad_msg.astype(jnp.bfloat16).reshape(-1, width)
    part_message = lax.dot_general(
        x_rows, grad_msg, (((0,), (0,)), ((), ())), preferred_element_type=jnp.float32
    )
    grad_features = (
        g_rows.astype(jnp.float32)
        + lax.dot_general(
            grad_msg, w_message, (((1,), (1,)), ((), ())), preferred_element_type=jnp.float32
        )
    ).astype(jnp.bfloat16)
    sum_message, sum_update = lax.psum((part_message, part_update), ("dp", "region"))
    scale = 1.0 / math.sqrt(lax.axis_size("dp") * lax.axis_size("region") * x_rows.shape[0])
    return (output[None], grad_features[None], sum_message * scale, sum_update * scale)


def solution(mesh):
    in_specs = (
        P(("groups", "dp"), "region", None),
        P(("groups", "dp"), "region", None, None),
        P(("groups", "dp"), "region"),
        P(("groups", "dp"), "region"),
        P(("groups", "dp"), "region"),
        P(("groups", "dp"), "region"),
        P(("groups", "dp"), "region"),
        P(),
        P(),
        P(("groups", "dp"), "region", None),
    )
    out_specs = (
        P(("groups", "dp"), "region", None),
        P(("groups", "dp"), "region", None),
        P("groups", None),
        P("groups", None),
    )
    return jax.shard_map(body, mesh=mesh, in_specs=in_specs, out_specs=out_specs, check_vma=False)
```

profile of v0, /device:TPU:1, one launch (start us, length us, event | category | flops | bytes accessed | tf_op | source)
XLA Modules:
  0.0 307.1 jit_solution(6473691448623572954)
XLA Ops:
  8.1 3.7 %convolution_convert_fusion.1 = bf16[4096,256]{1,0:T(8,128)(2,1)} fusion(bf16[256,256]{1,0:T(8,128)(2,1)} %param.17, bf16[1,4096,256]{2,1,0:T(8,128)(2,1)} %param.10), kind=kOutput, calls=%fused_computation.14 | convolution fusion | flops 537919488 | bytes 4325376 | tf_op jit(solution)/shard_map/dot_general | solution.py:44
  11.8 2.9 gather_fusion
  14.7 2.1 collective-permute-start
  16.8 2.9 gather_fusion.1
  19.7 2.0 collective-permute-start.1
  22.4 2.6 collective-permute-done
  25.1 6.4 %collective-permute-done.1 = bf16[4,128,256]{2,1,0:T(8,128)(2,1)S(1)} collective-permute-done((bf16[4,128,256]{2,1,0:T(8,128)(2,1)}, bf16[4,128,256]{2,1,0:T(8,128)(2,1)S(1)}, u32[]{:S(2)}, u32[]{:S(2)}) %collective-permute-start.1) | collective-permute-done | bytes 262176 | tf_op jit(solution)/shard_map/ppermute | solution.py:17
  31.4 3.5 %pad_maximum_fusion = bf16[40,128,256]{2,1,0:T(8,128)(2,1)} fusion(bf16[4,128,256]{2,1,0:T(8,128)(2,1)S(1)} %collective-permute-done.1, bf16[4,128,256]{2,1,0:T(8,128)(2,1)S(1)} %collective-permute-done, bf16[32,128,256]{2,1,0:T(8,128)(2,1)} %bitcast.66), kind=kLoop, calls=%fused_computation.22 | loop fusion | flops 2621440 | bytes 5242880 | tf_op jit(solution)/shard_map/concatenate | solution.py:49
  34.9 7.7 %gather_fusion.2 = bf16[96,128,256]{2,1,0:T(8,128)(2,1)} fusion(bf16[40,128,256]{2,1,0:T(8,128)(2,1)} %pad_maximum_fusion, s32[1024]{0:T(1024)S(1)} %pad_clamp_fusion.1), kind=kCustom, calls=%fused_computation.2 | custom fusion | bytes 12583296 | tf_op jit(solution)/shard_map/gather | solution.py:54
  42.6 9.8 %multiply_bitcast_fusion.1 = f32[96,128,256]{1,2,0:T(8,128)} fusion(f32[96]{0:T(128)S(1)} %compare_convert_fusion, bf16[96,128,256]{2,1,0:T(8,128)(2,1)} %gather_fusion.2, bf16[1,96,128,128]{3,2,1,0:T(8,128)(2,1)S(1)} %copy-done), kind=kOutput, calls=%fused_computation.9 | convolution fusion | flops 808452096 | bytes 22020480 | tf_op jit(solution)/shard_map/kij,kjd->kid/dot_general | solution.py:55
  52.5 12.6 %copy.20 = f32[96,128,256]{2,1,0:T(8,128)} copy(f32[96,128,256]{1,2,0:T(8,128)} %multiply_bitcast_fusion.1) | data formatting | bytes 25165824 | tf_op jit(solution)/shard_map/mul | solution.py:57
  65.1 2.4 broadcast_in_dim.8
  67.5 28.6 %scatter_fusion = f32[32,128,256]{2,1,0:T(8,128)} fusion(f32[32,128,256]{2,1,0:T(8,128)} %broadcast_in_dim.8, s32[96]{0:T(128)S(1)} %fusion.13, f32[96,128,256]{2,1,0:T(8,128)} %copy.20), kind=kCustom, calls=%fused_computation.4 | custom fusion | flops 3145728 | bytes 37749120 | tf_op jit(solution)/shard_map/scatter-add | solution.py:57
  96.1 2.6 convert_element_type.41
  99.6 3.6 %fusion.3 = (bf16[4096,256]{1,0:T(8,128)(2,1)S(1)}, bf16[1,4096,256]{2,1,0:T(8,128)(2,1)}) fusion(bf16[1,4096,256]{2,1,0:T(8,128)(2,1)S(1)} %copy-done.6, bf16[1,4096,256]{2,1,0:T(8,128)(2,1)S(1)} %copy-done.3, bf16[4096,256]{1,0:T(8,128)(2,1)S(1)} %bitcast.69, bf16[256,256]{1,0:T(8,128)(2,1)S(1)} %copy-done.10), kind=kOutput, calls=%fused_computation.17 | convolution fusion | flops 551550976 | bytes 10616832 | tf_op jit(solution)/shard_map/dot_general | solution.py:60
  104.5 2.1 convolution_convert_fusion
  106.6 7.6 %gather_fusion.3 = bf16[96,128,256]{2,1,0:T(8,128)(2,1)} fusion(bf16[32,128,256]{2,1,0:T(8,128)(2,1)} %bitcast.63, s32[1024]{0:T(1024)S(1)} %pad_clamp_fusion), kind=kCustom, calls=%fused_computation.3 | custom fusion | bytes 12583296 | tf_op jit(solution)/shard_map/gather | solution.py:72
  114.2 9.8 %multiply_bitcast_fusion = f32[96,128,256]{1,2,0:T(8,128)} fusion(f32[96]{0:T(128)S(1)} %compare_convert_fusion, bf16[96,128,256]{2,1,0:T(8,128)(2,1)} %gather_fusion.3, bf16[1,96,128,128]{3,2,1,0:T(8,128)(2,1)S(1)} %copy-done), kind=kOutput, calls=%fused_computation.8 | convolution fusion | flops 808452096 | bytes 22020480 | tf_op jit(solution)/shard_map/kij,kid->kjd/dot_general | solution.py:73
  124.0 12.6 %copy.22 = f32[96,128,256]{2,1,0:T(8,128)} copy(f32[96,128,256]{1,2,0:T(8,128)} %multiply_bitcast_fusion) | data formatting | bytes 25165824 | tf_op jit(solution)/shard_map/mul | solution.py:77
  136.6 2.9 broadcast_in_dim.10
  139.5 28.5 %scatter_fusion.1 = f32[40,128,256]{2,1,0:T(8,128)} fusion(f32[40,128,256]{2,1,0:T(8,128)} %broadcast_in_dim.10, s32[96]{0:T(128)S(1)} %fusion.16, f32[96,128,256]{2,1,0:T(8,128)} %copy.22), kind=kCustom, calls=%fused_computation.5 | custom fusion | flops 3145728 | bytes 37749120 | tf_op jit(solution)/shard_map/scatter-add | solution.py:77
  168.0 2.1 fusion.17
  170.5 2.8 collective-permute-start.3
  173.4 4.6 %slice.23 = f32[32,128,256]{2,1,0:T(8,128)} slice(f32[40,128,256]{2,1,0:T(8,128)} %scatter_fusion.1), slice={[0:32], [0:128], [0:256]} | slice | bytes 8388608 | tf_op jit(solution)/shard_map/slice | solution.py:83
  179.6 5.7 %collective-permute-done.2 = f32[4,128,256]{2,1,0:T(8,128)S(1)} collective-permute-done((f32[4,128,256]{2,1,0:T(8,128)S(1)}, f32[4,128,256]{2,1,0:T(8,128)S(1)}, u32[]{:S(2)}, u32[]{:S(2)}) %collective-permute-start.2) | collective-permute-done | bytes 524320 | tf_op jit(solution)/shard_map/ppermute | solution.py:15
  185.3 2.6 scatter_fusion.2
  188.0 6.7 %collective-permute-done.3 = f32[4,128,256]{2,1,0:T(8,128)S(1)} collective-permute-done((f32[4,128,256]{2,1,0:T(8,128)}, f32[4,128,256]{2,1,0:T(8,128)S(1)}, u32[]{:S(2)}, u32[]{:S(2)}) %collective-permute-start.3) | collective-permute-done | bytes 524320 | tf_op jit(solution)/shard_map/ppermute | solution.py:17
  194.7 2.6 scatter_fusion.3
  197.3 2.5 convert_element_type.47
  201.1 3.0 fusion.10
  204.2 4.4 %fusion.1 = bf16[1,4096,256]{2,1,0:T(8,128)(2,1)} fusion(bf16[4096,256]{1,0:T(8,128)(2,1)} %bitcast.68, bf16[256,256]{1,0:T(8,128)(2,1)S(1)} %copy-done.9, bf16[1,4096,256]{2,1,0:T(8,128)(2,1)} %param.19), kind=kOutput, calls=%fused_computation.15 | convolution fusion | flops 540016640 | bytes 6422528 | tf_op jit(solution)/shard_map/dot_general | solution.py:92
  208.6 87.2 %all-reduce.3.cloned.1.call-done = (f32[256,256]{0,1:T(8,128)}, f32[256,256]{0,1:T(8,128)}) async-done(((f32[256,256]{0,1:T(8,128)}, f32[256,256]{0,1:T(8,128)}), (f32[256,256]{0,1:T(8,128)}, f32[256,256]{0,1:T(8,128)})) %all-reduce.3.cloned.1.call-update) | async-done | bytes 524304 | tf_op jit(solution)/shard_map/psum | solution.py:96
  (44 shorter events, 10.9 us)
Async XLA Ops:
  7.2 35.5 %copy-start = (bf16[1,96,128,128]{3,2,1,0:T(8,128)(2,1)S(1)}, bf16[1,96,128,128]{3,2,1,0:T(8,128)(2,1)}, u32[]{:S(2)}) copy-start(bf16[1,96,128,128]{3,2,1,0:T(8,128)(2,1)} %param.11) | copy-start | bytes 9437188
  7.2 9.6 %copy-start.11 = (s32[1,4]{1,0:T(1,128)S(1)}, s32[1,4]{1,0:T(1,128)}, u32[]{:S(2)}) copy-start(s32[1,4]{1,0:T(1,128)} %param.15) | copy-start | bytes 52
  7.2 14.5 %copy-start.12 = (s32[1,96]{1,0:T(1,128)S(1)}, s32[1,96]{1,0:T(1,128)}, u32[]{:S(2)}) copy-start(s32[1,96]{1,0:T(1,128)} %param.12) | copy-start | bytes 1156
  7.2 15.2 %copy-start.13 = (s32[1,96]{1,0:T(1,128)S(1)}, s32[1,96]{1,0:T(1,128)}, u32[]{:S(2)}) copy-start(s32[1,96]{1,0:T(1,128)} %param.13) | copy-start | bytes 1156
  7.2 288.6 %all-reduce.3.cloned.1.call-start = ((), (), s32[]{:S(2)}) async-start(), calls=%async_computation | async-start | bytes 1048576 | tf_op jit(solution)/shard_map/psum | solution.py:96
  14.7 10.4 %collective-permute-start = (bf16[4,128,256]{2,1,0:T(8,128)(2,1)}, bf16[4,128,256]{2,1,0:T(8,128)(2,1)S(1)}, u32[]{:S(2)}, u32[]{:S(2)}) collective-permute-start(bf16[4,128,256]{2,1,0:T(8,128)(2,1)} %gather_fusion), channel_id=1, source_target_pairs={{0,1},{1,2},{2,3},{3,0},{4,5},{5,6},{6,7},{7,4},{8,9},{9,10},{10,1... | collective-permute-start | bytes 786440 | tf_op jit(solution)/shard_map/ppermute | solution.py:15
  19.7 11.7 %collective-permute-start.1 = (bf16[4,128,256]{2,1,0:T(8,128)(2,1)}, bf16[4,128,256]{2,1,0:T(8,128)(2,1)S(1)}, u32[]{:S(2)}, u32[]{:S(2)}) collective-permute-start(bf16[4,128,256]{2,1,0:T(8,128)(2,1)} %gather_fusion.1), channel_id=1, source_target_pairs={{1,0},{2,1},{3,2},{0,3},{5,4},{6,5},{7,6},{4,7},{9,8},{10,9},{11,1... | collective-permute-start | bytes 786440 | tf_op jit(solution)/shard_map/ppermute | solution.py:17
  96.1 2.9 copy-start.3
  96.1 3.5 %copy-start.6 = (bf16[1,4096,256]{2,1,0:T(8,128)(2,1)S(1)}, bf16[1,4096,256]{2,1,0:T(8,128)(2,1)}, u32[]{:S(2)}) copy-start(bf16[1,4096,256]{2,1,0:T(8,128)(2,1)} %param.19) | copy-start | bytes 6291460
  96.1 3.5 %copy-start.10 = (bf16[256,256]{1,0:T(8,128)(2,1)S(1)}, bf16[256,256]{1,0:T(8,128)(2,1)}, u32[]{:S(2)}) copy-start(bf16[256,256]{1,0:T(8,128)(2,1)} %param.18) | copy-start | bytes 393220
  98.7 4.5 %copy-start.7 = (bf16[32,128,256]{2,1,0:T(8,128)(2,1)}, bf16[32,128,256]{2,1,0:T(8,128)(2,1)S(1)}, u32[]{:S(2)}) copy-start(bf16[32,128,256]{2,1,0:T(8,128)(2,1)S(1)} %convert_element_type.41) | copy-start | bytes 6291460
  103.2 1.3 copy-start.4
  170.1 15.2 %collective-permute-start.2 = (f32[4,128,256]{2,1,0:T(8,128)S(1)}, f32[4,128,256]{2,1,0:T(8,128)S(1)}, u32[]{:S(2)}, u32[]{:S(2)}) collective-permute-start(f32[4,128,256]{2,1,0:T(8,128)S(1)} %get-tuple-element.15), channel_id=1, source_target_pairs={{0,1},{1,2},{2,3},{3,0},{4,5},{5,6},{6,7},{7,4},{8,9},{9,10},{10,1... | collective-permute-start | bytes 1572872 | tf_op jit(solution)/shard_map/ppermute | solution.py:15
  170.5 7.4 %copy-start.5 = (bf16[4096,256]{1,0:T(8,128)(2,1)S(1)}, bf16[4096,256]{1,0:T(8,128)(2,1)}, u32[]{:S(2)}) copy-start(bf16[4096,256]{1,0:T(8,128)(2,1)} %copy-done.4) | copy-start | bytes 6291460
  170.5 7.4 %copy-start.8 = (bf16[32,128,256]{2,1,0:T(8,128)(2,1)S(1)}, bf16[32,128,256]{2,1,0:T(8,128)(2,1)}, u32[]{:S(2)}) copy-start(bf16[32,128,256]{2,1,0:T(8,128)(2,1)} %copy-done.7) | copy-start | bytes 6291460
  170.5 24.1 %collective-permute-start.3 = (f32[4,128,256]{2,1,0:T(8,128)}, f32[4,128,256]{2,1,0:T(8,128)S(1)}, u32[]{:S(2)}, u32[]{:S(2)}) collective-permute-start(f32[4,128,256]{2,1,0:T(8,128)} %get-tuple-element.14), channel_id=1, source_target_pairs={{1,0},{2,1},{3,2},{0,3},{5,4},{6,5},{7,6},{4,7},{9,8},{10,9},{11,1... | collective-permute-start | bytes 1572872 | tf_op jit(solution)/shard_map/ppermute | solution.py:17
  199.8 1.3 copy-start.2
  199.8 4.4 %copy-start.9 = (bf16[256,256]{1,0:T(8,128)(2,1)S(1)}, bf16[256,256]{1,0:T(8,128)(2,1)}, u32[]{:S(2)}) copy-start(bf16[256,256]{1,0:T(8,128)(2,1)} %param.17) | copy-start | bytes 393220
  204.2 96.1 %copy-start.1 = (bf16[1,96,128,128]{3,2,1,0:T(8,128)(2,1)S(1)}, bf16[1,96,128,128]{3,2,1,0:T(8,128)(2,1)}, u32[]{:S(2)}) copy-start(bf16[1,96,128,128]{3,2,1,0:T(8,128)(2,1)} %param.11) | copy-start | bytes 9437188
Sparse Core Ops, SparseCore 0:
  204.3 91.5 all-reduce.2
where the time goes:
time: 308 us; the launch traced here: 307 us
  waiting for transfers between devices  109 us (35%)
  other arithmetic  73.6 us (24%)
  local copies, waits for them, and re-layouts  64.3 us (21%)
  matrix products  38.2 us (12%)
  between operations  14.8 us (5%)
  starting transfers between devices  7.47 us (2%)
    psum x1, waiting for transfers between devices, body(): lax.psum((part_message, part_update), ('dp', 'region'))  87.2 us
    scatter-add x1, other arithmetic, body(): jnp.zeros((ntile, tile, width), jnp.float32).at[dst]  28.6 us
    scatter-add x1, other arithmetic, body(): grad_ext = jnp.zeros((ntile + 2 * bound, tile, width), jnp.float32).at[sr...  28.5 us
    ppermute x2, waiting for transfers between devices, with_halo(): lax.ppermute(head, axis, [((i + 1) % count, i) for i in range(count)])  13 us
    mul x1, local copies, waits for them, and re-layouts, body(): contrib * live[:, None, None]  12.6 us
    mul x1, local copies, waits for them, and re-layouts, body(): back * live[:, None, None]  12.6 us
    dot_general x1, matrix products, body(): jnp.einsum('kij,kjd->kid', adj, gathered, preferred_element_type=jnp.floa...  9.84 us
    dot_general x1, matrix products, body(): jnp.einsum('kij,kid->kjd', adj, picked, preferred_element_type=jnp.float32)  9.84 us
  transfers between devices with their start and end apart: 5, of which 5 were waited for; matrix products, arithmetic and copies ran while one was open for 5% of the time, Pallas kernels for 0%

commit v1 on v0

--- a/solution.py
+++ b/solution.py
@@ -93,7 +93,7 @@
             grad_msg, w_message, (((1,), (1,)), ((), ())), preferred_element_type=jnp.float32
         )
     ).astype(jnp.bfloat16)
-    sum_message, sum_update = lax.psum((part_message, part_update), ("dp", "region"))
+    sum_message, sum_update = lax.psum(lax.psum((part_message, part_update), "region"), "dp")
     scale = 1.0 / math.sqrt(lax.axis_size("dp") * lax.axis_size("region") * x_rows.shape[0])
     return (output[None], grad_features[None], sum_message * scale, sum_update * scale)
 

time: 308 us -> 292 us (0.948)
  waiting for transfers between devices: 109 us -> 90.5 us
    psum x1 -> x2, waiting for transfers between devices: 87.2 us -> 69.3 us  [the longest x1 38.5 us: body(): lax.psum((part_message, part_update), 'region')]
  transfers between devices with their start and end apart: 5 -> 6, of which waited for: 5 -> 6; matrix products, arithmetic and copies ran while one was open for 5% -> 6% of each run, Pallas kernels for 0% -> 0%
where the time goes in v1:
time: 292 us; the launch traced here: 289 us
  waiting for transfers between devices  90.5 us (31%)
  other arithmetic  73.8 us (25%)
  local copies, waits for them, and re-layouts  64.4 us (22%)
  matrix products  38.2 us (13%)
  between operations  14.8 us (5%)
  starting transfers between devices  7.51 us (3%)
    psum x1, waiting for transfers between devices, body(): lax.psum((part_message, part_update), 'region')  38.5 us
    psum x1, waiting for transfers between devices, body(): lax.psum(lax.psum((part_message, part_update), 'region'), 'dp')  30.8 us
    scatter-add x1, other arithmetic, body(): grad_ext = jnp.zeros((ntile + 2 * bound, tile, width), jnp.float32).at[sr...  28.7 us
    scatter-add x1, other arithmetic, body(): jnp.zeros((ntile, tile, width), jnp.float32).at[dst]  28.6 us
    ppermute x2, waiting for transfers between devices, with_halo(): lax.ppermute(head, axis, [((i + 1) % count, i) for i in range(count)])  12.6 us
    mul x1, local copies, waits for them, and re-layouts, body(): contrib * live[:, None, None]  12.6 us
    mul x1, local copies, waits for them, and re-layouts, body(): back * live[:, None, None]  12.6 us
    dot_general x1, matrix products, body(): jnp.einsum('kij,kjd->kid', adj, gathered, preferred_element_type=jnp.floa...  9.85 us
  transfers between devices with their start and end apart: 6, of which 6 were waited for; matrix products, arithmetic and copies ran while one was open for 6% of the time, Pallas kernels for 0%

profile of v1, /device:TPU:1, one launch (start us, length us, event | category | flops | bytes accessed | tf_op | source)
XLA Modules:
  0.0 289.2 jit_solution(12038763260572393632)
XLA Ops:
  8.1 3.7 %convolution_convert_fusion.1 = bf16[4096,256]{1,0:T(8,128)(2,1)} fusion(bf16[256,256]{1,0:T(8,128)(2,1)} %param.17, bf16[1,4096,256]{2,1,0:T(8,128)(2,1)} %param.10), kind=kOutput, calls=%fused_computation.14 | convolution fusion | flops 537919488 | bytes 4325376 | tf_op jit(solution)/shard_map/dot_general | solution.py:44
  11.8 2.9 gather_fusion
  14.7 2.1 collective-permute-start
  16.8 2.9 gather_fusion.1
  22.4 2.6 collective-permute-done
  25.1 6.4 %collective-permute-done.1 = bf16[4,128,256]{2,1,0:T(8,128)(2,1)S(1)} collective-permute-done((bf16[4,128,256]{2,1,0:T(8,128)(2,1)}, bf16[4,128,256]{2,1,0:T(8,128)(2,1)S(1)}, u32[]{:S(2)}, u32[]{:S(2)}) %collective-permute-start.1) | collective-permute-done | bytes 262176 | tf_op jit(solution)/shard_map/ppermute | solution.py:17
  31.4 3.5 %pad_maximum_fusion = bf16[40,128,256]{2,1,0:T(8,128)(2,1)} fusion(bf16[4,128,256]{2,1,0:T(8,128)(2,1)S(1)} %collective-permute-done.1, bf16[4,128,256]{2,1,0:T(8,128)(2,1)S(1)} %collective-permute-done, bf16[32,128,256]{2,1,0:T(8,128)(2,1)} %bitcast.66), kind=kLoop, calls=%fused_computation.22 | loop fusion | flops 2621440 | bytes 5242880 | tf_op jit(solution)/shard_map/concatenate | solution.py:49
  34.9 7.7 %gather_fusion.2 = bf16[96,128,256]{2,1,0:T(8,128)(2,1)} fusion(bf16[40,128,256]{2,1,0:T(8,128)(2,1)} %pad_maximum_fusion, s32[1024]{0:T(1024)S(1)} %pad_clamp_fusion.1), kind=kCustom, calls=%fused_computation.2 | custom fusion | bytes 12583296 | tf_op jit(solution)/shard_map/gather | solution.py:54
  42.6 9.9 %multiply_bitcast_fusion.1 = f32[96,128,256]{1,2,0:T(8,128)} fusion(f32[96]{0:T(128)S(1)} %compare_convert_fusion, bf16[96,128,256]{2,1,0:T(8,128)(2,1)} %gather_fusion.2, bf16[1,96,128,128]{3,2,1,0:T(8,128)(2,1)S(1)} %copy-done), kind=kOutput, calls=%fused_computation.9 | convolution fusion | flops 808452096 | bytes 22020480 | tf_op jit(solution)/shard_map/kij,kjd->kid/dot_general | solution.py:55
  52.5 12.6 %copy.20 = f32[96,128,256]{2,1,0:T(8,128)} copy(f32[96,128,256]{1,2,0:T(8,128)} %multiply_bitcast_fusion.1) | data formatting | bytes 25165824 | tf_op jit(solution)/shard_map/mul | solution.py:57
  65.0 2.4 broadcast_in_dim.8
  67.5 28.6 %scatter_fusion = f32[32,128,256]{2,1,0:T(8,128)} fusion(f32[32,128,256]{2,1,0:T(8,128)} %broadcast_in_dim.8, s32[96]{0:T(128)S(1)} %fusion.13, f32[96,128,256]{2,1,0:T(8,128)} %copy.20), kind=kCustom, calls=%fused_computation.4 | custom fusion | flops 3145728 | bytes 37749120 | tf_op jit(solution)/shard_map/scatter-add | solution.py:57
  96.1 2.6 convert_element_type.41
  99.6 3.6 %fusion.3 = (bf16[4096,256]{1,0:T(8,128)(2,1)S(1)}, bf16[1,4096,256]{2,1,0:T(8,128)(2,1)}) fusion(bf16[1,4096,256]{2,1,0:T(8,128)(2,1)S(1)} %copy-done.6, bf16[1,4096,256]{2,1,0:T(8,128)(2,1)S(1)} %copy-done.3, bf16[4096,256]{1,0:T(8,128)(2,1)S(1)} %bitcast.69, bf16[256,256]{1,0:T(8,128)(2,1)S(1)} %copy-done.10), kind=kOutput, calls=%fused_computation.17 | convolution fusion | flops 551550976 | bytes 10616832 | tf_op jit(solution)/shard_map/dot_general | solution.py:60
  104.5 2.1 convolution_convert_fusion
  106.6 7.6 %gather_fusion.3 = bf16[96,128,256]{2,1,0:T(8,128)(2,1)} fusion(bf16[32,128,256]{2,1,0:T(8,128)(2,1)} %bitcast.63, s32[1024]{0:T(1024)S(1)} %pad_clamp_fusion), kind=kCustom, calls=%fused_computation.3 | custom fusion | bytes 12583296 | tf_op jit(solution)/shard_map/gather | solution.py:72
  114.2 9.9 %multiply_bitcast_fusion = f32[96,128,256]{1,2,0:T(8,128)} fusion(f32[96]{0:T(128)S(1)} %compare_convert_fusion, bf16[96,128,256]{2,1,0:T(8,128)(2,1)} %gather_fusion.3, bf16[1,96,128,128]{3,2,1,0:T(8,128)(2,1)S(1)} %copy-done), kind=kOutput, calls=%fused_computation.8 | convolution fusion | flops 808452096 | bytes 22020480 | tf_op jit(solution)/shard_map/kij,kid->kjd/dot_general | solution.py:73
  124.1 12.6 %copy.22 = f32[96,128,256]{2,1,0:T(8,128)} copy(f32[96,128,256]{1,2,0:T(8,128)} %multiply_bitcast_fusion) | data formatting | bytes 25165824 | tf_op jit(solution)/shard_map/mul | solution.py:77
  136.6 2.9 broadcast_in_dim.10
  139.5 28.7 %scatter_fusion.1 = f32[40,128,256]{2,1,0:T(8,128)} fusion(f32[40,128,256]{2,1,0:T(8,128)} %broadcast_in_dim.10, s32[96]{0:T(128)S(1)} %fusion.16, f32[96,128,256]{2,1,0:T(8,128)} %copy.22), kind=kCustom, calls=%fused_computation.5 | custom fusion | flops 3145728 | bytes 37749120 | tf_op jit(solution)/shard_map/scatter-add | solution.py:77
  168.2 2.1 fusion.17
  170.6 3.0 %collective-permute-start.3 = (f32[4,128,256]{2,1,0:T(8,128)}, f32[4,128,256]{2,1,0:T(8,128)S(1)}, u32[]{:S(2)}, u32[]{:S(2)}) collective-permute-start(f32[4,128,256]{2,1,0:T(8,128)} %get-tuple-element.16), channel_id=1, source_target_pairs={{1,0},{2,1},{3,2},{0,3},{5,4},{6,5},{7,6},{4,7},{9,8},{10,9},{11,1... | collective-permute-start | bytes 1572872 | tf_op jit(solution)/shard_map/ppermute | solution.py:17
  173.6 4.6 %slice.23 = f32[32,128,256]{2,1,0:T(8,128)} slice(f32[40,128,256]{2,1,0:T(8,128)} %scatter_fusion.1), slice={[0:32], [0:128], [0:256]} | slice | bytes 8388608 | tf_op jit(solution)/shard_map/slice | solution.py:83
  179.8 5.9 %collective-permute-done.2 = f32[4,128,256]{2,1,0:T(8,128)S(1)} collective-permute-done((f32[4,128,256]{2,1,0:T(8,128)S(1)}, f32[4,128,256]{2,1,0:T(8,128)S(1)}, u32[]{:S(2)}, u32[]{:S(2)}) %collective-permute-start.2) | collective-permute-done | bytes 524320 | tf_op jit(solution)/shard_map/ppermute | solution.py:15
  185.7 2.7 scatter_fusion.2
  188.4 6.3 %collective-permute-done.3 = f32[4,128,256]{2,1,0:T(8,128)S(1)} collective-permute-done((f32[4,128,256]{2,1,0:T(8,128)}, f32[4,128,256]{2,1,0:T(8,128)S(1)}, u32[]{:S(2)}, u32[]{:S(2)}) %collective-permute-start.3) | collective-permute-done | bytes 524320 | tf_op jit(solution)/shard_map/ppermute | solution.py:17
  194.6 2.7 scatter_fusion.3
  197.3 2.5 convert_element_type.47
  201.1 3.0 %fusion.10 = f32[256,256]{0,1:T(8,128)} fusion(bf16[4096,256]{1,0:T(8,128)(2,1)S(1)} %bitcast.67, bf16[1,4096,256]{2,1,0:T(8,128)(2,1)} %param.10), kind=kOutput, calls=%fused_computation.27 | convolution fusion | flops 536870912 | bytes 4456448 | tf_op jit(solution)/shard_map/dot_general | solution.py:87
  204.2 38.5 %all-reduce.5.cloned.1.call-done = (f32[256,256]{0,1:T(8,128)}, f32[256,256]{0,1:T(8,128)}) async-done(((f32[256,256]{0,1:T(8,128)}, f32[256,256]{0,1:T(8,128)}), (f32[256,256]{0,1:T(8,128)}, f32[256,256]{0,1:T(8,128)})) %all-reduce.5.cloned.1.call-update) | async-done | bytes 524304 | tf_op jit(solution)/shard_map/psum | solution.py:96
  242.7 4.4 %fusion.1 = bf16[1,4096,256]{2,1,0:T(8,128)(2,1)} fusion(bf16[4096,256]{1,0:T(8,128)(2,1)} %bitcast.68, bf16[256,256]{1,0:T(8,128)(2,1)S(1)} %copy-done.9, bf16[1,4096,256]{2,1,0:T(8,128)(2,1)} %param.19), kind=kOutput, calls=%fused_computation.15 | convolution fusion | flops 540016640 | bytes 6422528 | tf_op jit(solution)/shard_map/dot_general | solution.py:92
  247.2 30.8 %all-reduce.7.cloned.1.call-done = (f32[256,256]{0,1:T(8,128)}, f32[256,256]{0,1:T(8,128)}) async-done(((f32[256,256]{0,1:T(8,128)}, f32[256,256]{0,1:T(8,128)}), (f32[256,256]{0,1:T(8,128)}, f32[256,256]{0,1:T(8,128)})) %all-reduce.7.cloned.1.call-update) | async-done | bytes 524304 | tf_op jit(solution)/shard_map/psum | solution.py:96
  (47 shorter events, 12.8 us)
Async XLA Ops:
  7.2 35.4 %copy-start = (bf16[1,96,128,128]{3,2,1,0:T(8,128)(2,1)S(1)}, bf16[1,96,128,128]{3,2,1,0:T(8,128)(2,1)}, u32[]{:S(2)}) copy-start(bf16[1,96,128,128]{3,2,1,0:T(8,128)(2,1)} %param.11) | copy-start | bytes 9437188
  7.2 9.6 %copy-start.11 = (s32[1,4]{1,0:T(1,128)S(1)}, s32[1,4]{1,0:T(1,128)}, u32[]{:S(2)}) copy-start(s32[1,4]{1,0:T(1,128)} %param.15) | copy-start | bytes 52
  7.2 14.5 %copy-start.12 = (s32[1,96]{1,0:T(1,128)S(1)}, s32[1,96]{1,0:T(1,128)}, u32[]{:S(2)}) copy-start(s32[1,96]{1,0:T(1,128)} %param.12) | copy-start | bytes 1156
  7.2 15.2 %copy-start.13 = (s32[1,96]{1,0:T(1,128)S(1)}, s32[1,96]{1,0:T(1,128)}, u32[]{:S(2)}) copy-start(s32[1,96]{1,0:T(1,128)} %param.13) | copy-start | bytes 1156
  7.2 235.5 %all-reduce.5.cloned.1.call-start = ((), (), s32[]{:S(2)}) async-start(), calls=%async_computation | async-start | bytes 1048576 | tf_op jit(solution)/shard_map/psum | solution.py:96
  14.7 10.4 %collective-permute-start = (bf16[4,128,256]{2,1,0:T(8,128)(2,1)}, bf16[4,128,256]{2,1,0:T(8,128)(2,1)S(1)}, u32[]{:S(2)}, u32[]{:S(2)}) collective-permute-start(bf16[4,128,256]{2,1,0:T(8,128)(2,1)} %gather_fusion), channel_id=1, source_target_pairs={{0,1},{1,2},{2,3},{3,0},{4,5},{5,6},{6,7},{7,4},{8,9},{9,10},{10,1... | collective-permute-start | bytes 786440 | tf_op jit(solution)/shard_map/ppermute | solution.py:15
  19.7 11.7 %collective-permute-start.1 = (bf16[4,128,256]{2,1,0:T(8,128)(2,1)}, bf16[4,128,256]{2,1,0:T(8,128)(2,1)S(1)}, u32[]{:S(2)}, u32[]{:S(2)}) collective-permute-start(bf16[4,128,256]{2,1,0:T(8,128)(2,1)} %gather_fusion.1), channel_id=1, source_target_pairs={{1,0},{2,1},{3,2},{0,3},{5,4},{6,5},{7,6},{4,7},{9,8},{10,9},{11,1... | collective-permute-start | bytes 786440 | tf_op jit(solution)/shard_map/ppermute | solution.py:17
  96.1 2.9 copy-start.3
  96.1 3.5 %copy-start.6 = (bf16[1,4096,256]{2,1,0:T(8,128)(2,1)S(1)}, bf16[1,4096,256]{2,1,0:T(8,128)(2,1)}, u32[]{:S(2)}) copy-start(bf16[1,4096,256]{2,1,0:T(8,128)(2,1)} %param.19) | copy-start | bytes 6291460
  96.1 3.5 %copy-start.10 = (bf16[256,256]{1,0:T(8,128)(2,1)S(1)}, bf16[256,256]{1,0:T(8,128)(2,1)}, u32[]{:S(2)}) copy-start(bf16[256,256]{1,0:T(8,128)(2,1)} %param.18) | copy-start | bytes 393220
  98.7 4.5 %copy-start.7 = (bf16[32,128,256]{2,1,0:T(8,128)(2,1)}, bf16[32,128,256]{2,1,0:T(8,128)(2,1)S(1)}, u32[]{:S(2)}) copy-start(bf16[32,128,256]{2,1,0:T(8,128)(2,1)S(1)} %convert_element_type.41) | copy-start | bytes 6291460
  103.2 1.3 copy-start.4
  170.3 15.4 %collective-permute-start.2 = (f32[4,128,256]{2,1,0:T(8,128)S(1)}, f32[4,128,256]{2,1,0:T(8,128)S(1)}, u32[]{:S(2)}, u32[]{:S(2)}) collective-permute-start(f32[4,128,256]{2,1,0:T(8,128)S(1)} %get-tuple-element.17), channel_id=1, source_target_pairs={{0,1},{1,2},{2,3},{3,0},{4,5},{5,6},{6,7},{7,4},{8,9},{9,10},{10,1... | collective-permute-start | bytes 1572872 | tf_op jit(solution)/shard_map/ppermute | solution.py:15
  170.6 7.6 %copy-start.5 = (bf16[4096,256]{1,0:T(8,128)(2,1)S(1)}, bf16[4096,256]{1,0:T(8,128)(2,1)}, u32[]{:S(2)}) copy-start(bf16[4096,256]{1,0:T(8,128)(2,1)} %copy-done.4) | copy-start | bytes 6291460
  170.6 7.6 %copy-start.8 = (bf16[32,128,256]{2,1,0:T(8,128)(2,1)S(1)}, bf16[32,128,256]{2,1,0:T(8,128)(2,1)}, u32[]{:S(2)}) copy-start(bf16[32,128,256]{2,1,0:T(8,128)(2,1)} %copy-done.7) | copy-start | bytes 6291460
  170.6 24.1 %collective-permute-start.3 = (f32[4,128,256]{2,1,0:T(8,128)}, f32[4,128,256]{2,1,0:T(8,128)S(1)}, u32[]{:S(2)}, u32[]{:S(2)}) collective-permute-start(f32[4,128,256]{2,1,0:T(8,128)} %get-tuple-element.16), channel_id=1, source_target_pairs={{1,0},{2,1},{3,2},{0,3},{5,4},{6,5},{7,6},{4,7},{9,8},{10,9},{11,1... | collective-permute-start | bytes 1572872 | tf_op jit(solution)/shard_map/ppermute | solution.py:17
  199.7 1.3 copy-start.2
  199.8 42.9 %copy-start.9 = (bf16[256,256]{1,0:T(8,128)(2,1)S(1)}, bf16[256,256]{1,0:T(8,128)(2,1)}, u32[]{:S(2)}) copy-start(bf16[256,256]{1,0:T(8,128)(2,1)} %param.17) | copy-start | bytes 393220
  204.1 73.8 %all-reduce.7.cloned.1.call-start = ((), (), s32[]{:S(2)}) async-start(), calls=%async_computation.1 | async-start | bytes 1048576 | tf_op jit(solution)/shard_map/psum | solution.py:96
  242.7 39.7 %copy-start.1 = (bf16[1,96,128,128]{3,2,1,0:T(8,128)(2,1)S(1)}, bf16[1,96,128,128]{3,2,1,0:T(8,128)(2,1)}, u32[]{:S(2)}) copy-start(bf16[1,96,128,128]{3,2,1,0:T(8,128)(2,1)} %param.11) | copy-start | bytes 9437188
Sparse Core Ops, SparseCore 0:
  204.3 38.3 all-reduce.4
  245.1 32.8 all-reduce.6
